TPU v7x, 32 devices: a whole 2x2x4 slice. The times are simulated.
32 devices in a mesh: dom: 8 (over z, core), rep: 4 (over y, x).
Axes of the slice: x: 2, y: 2, z: 4, core: 2. Of those that a mesh axis runs over, the one named last changes fastest.
Arguments:
- node_features: bfloat16 [16384, 256], P(('dom', 'rep')), may hold values from -6 to 6
- weight: bfloat16 [256, 256], replicated, may hold values from -0.375 to 0.375
- cotangent: bfloat16 [16384, 256], P(('dom', 'rep')), may hold values from -6 to 6
- tile_row: int32 [8, 4, 512], P('dom', 'rep'), may hold values from 0 to 15
- tile_col: int32 [8, 4, 512], P('dom', 'rep'), may hold values from 0 to 31
- tile_values: bfloat16 [8, 4, 512, 128, 128], P('dom', 'rep'), may hold values from -0.0625 to 0.0625
- tile_count: int32 [8, 4], P('dom', 'rep'), may hold values from 128 to 512, as said below
Outputs:
- output: bfloat16 [16384, 256], P(('dom', 'rep'))
- grad_features: bfloat16 [16384, 256], P(('dom', 'rep'))
- grad_weight: float32 [256, 256], replicated
Inputs may be any that keep to these rules, and one draw needn't show every extreme that they name: Live slots are the first tile_count slots of each device's list; some device has all 512 slots live.
All inputs are finite; a program needn't handle non-finite values.
Results may differ from a plain program's by a relative error of at most 0.0061.
Values may be sent and summed in bfloat16 or wider, within the bound.
A program may use at most 192 MiB of HBM per device.

v0:
```python
import functools

import jax
import jax.numpy as jnp
from jax import lax
from jax.experimental import pallas as pl
from jax.experimental.pallas import tpu as pltpu
from jax.sharding import PartitionSpec as P

LOADS = 8
SUB = 2
SPLIT = 4
TILE = 128
MESH = pl.DeviceIdType.MESH


def order_tiles(count, row, col, col_blocks, order_out, place_out, last_out):
    slots, places = order_out.shape[1], last_out.shape[1]
    square = (TILE, TILE)
    lane = lax.broadcasted_iota(jnp.int32, (1, slots), 1)
    spot = jnp.where(lane < count, row * col_blocks + col, places)
    key = (spot * slots + lane).astype(jnp.float32)
    spot = spot.astype(jnp.float32)
    across = lax.broadcasted_iota(jnp.int32, square, 1).astype(jnp.float32)
    down = lax.broadcasted_iota(jnp.int32, square, 0).astype(jnp.float32)
    ones = jnp.ones(square, jnp.bfloat16)
    groups = slots // TILE
    zero = jnp.zeros(square, jnp.float32)

    def wide(values, q):
        return jnp.broadcast_to(values[:, q * TILE : (q + 1) * TILE], square)

    tall_spot, rank = [], []
    for q in range(groups):
        tall_key = jnp.transpose(wide(key, q))
        tall_spot.append(jnp.transpose(wide(spot, q)))
        ahead = zero
        for j in range(groups):
            ahead = ahead + jnp.where(wide(key, j) < tall_key, 1.0, 0.0)
        rank.append(jnp.dot(ahead.astype(jnp.bfloat16), ones, preferred_element_type=jnp.float32))
    for r in range(groups):
        want = across + float(r * TILE)
        slot, place = zero, zero
        for q in range(groups):
            hit = rank[q] == want
            slot = slot + jnp.where(hit, down + float(q * TILE), 0.0)
            place = place + jnp.where(hit, tall_spot[q], 0.0)
        order_out[:, pl.ds(r * TILE, TILE)] = jnp.sum(slot, axis=0, keepdims=True).astype(jnp.int32)
        place_out[:, pl.ds(r * TILE, TILE)] = jnp.sum(place, axis=0, keepdims=True).astype(jnp.int32)
    for p in range(places // TILE):
        want = across + float(p * TILE)
        upto, here = zero, zero
        for q in range(groups):
            upto = upto + jnp.where(tall_spot[q] <= want, 1.0, 0.0)
            here = here + jnp.where(tall_spot[q] == want, 1.0, 0.0)
        upto = jnp.sum(upto, axis=0, keepdims=True)
        here = jnp.sum(here, axis=0, keepdims=True)
        last_out[:, pl.ds(p * TILE, TILE)] = jnp.where(here > 0.0, upto - 1.0, float(slots)).astype(jnp.int32)


def layer_kernel(dom_size, rep_size, *refs):
    chips = dom_size // 2
    (
        count_ref, x_hbm, weight_hbm, cot_hbm, row_hbm, col_hbm, tiles_hbm, out_ref, gp_ref, gw_ref,
        source, raw, scan, weight_ref, cot_ref, row_v, col_v, order_v, place_v, last_v, order, place, last,
        part_send, part_recv, held, grads, back, pair, up_send, up_recv, down_send, down_recv,
        gw1_send, gw1_recv, gw2_send, gw2_recv, gw3_recv,
        raw_sem, small_sem, table_sem, lift_ssem, lift_rsem, sink_ssem, sink_rsem, share_ssem, share_rsem,
        part_ssem, part_rsem, grad_ssem, grad_rsem, pair_ssem, pair_rsem, up_ssem, up_rsem, down_ssem, down_rsem,
        gw1_ssem, gw1_rsem, gw2_ssem, gw2_rsem, gw3_ssem, gw3_rsem,
    ) = refs
    rows, width = cot_ref.shape
    slots = raw.shape[0]
    blocks = rows // TILE
    col_blocks = dom_size * blocks
    me_d, me_r = lax.axis_index("dom"), lax.axis_index("rep")
    chip, core = me_d // 2, lax.rem(me_d, 2)
    partner = chip * 2 + 1 - core
    share = width // dom_size

    def dom_peer(i):
        return lax.rem(me_d + i, dom_size)

    def rep_peer(i):
        return lax.rem(me_r + i, rep_size)

    barrier = pltpu.get_barrier_semaphore()
    for i in range(1, dom_size):
        pl.semaphore_signal(barrier, inc=1, device_id=(dom_peer(i), me_r), device_id_type=MESH)
    for i in range(1, rep_size):
        pl.semaphore_signal(barrier, inc=1, device_id=(me_d, rep_peer(i)), device_id_type=MESH)

    small = [
        pltpu.make_async_copy(row_hbm, row_v, small_sem.at[0]),
        pltpu.make_async_copy(col_hbm, col_v, small_sem.at[1]),
        pltpu.make_async_copy(
            x_hbm, source.at[pl.ds(pl.multiple_of(me_d * rows, rows), rows)], small_sem.at[2]
        ),
        pltpu.make_async_copy(weight_hbm, weight_ref, small_sem.at[3]),
        pltpu.make_async_copy(cot_hbm, cot_ref, small_sem.at[4]),
    ]
    for copy in small:
        copy.start()
    per_load = slots // LOADS
    loads = [
        pltpu.make_async_copy(
            tiles_hbm.at[pl.ds(c * per_load, per_load)], raw.at[pl.ds(c * per_load, per_load)], raw_sem.at[c]
        )
        for c in range(LOADS)
    ]
    for copy in loads:
        copy.start()

    step = rows // SUB

    def lines_of(s, side, b):
        return pl.ds(pl.multiple_of((s * 2 + side) * rows + b * step, step), step)

    def hop(n, b, s, to, ssem, rsem):
        here = x_hbm.at[pl.ds(b * step, step)] if n == 0 else source.at[lines_of(s, core, b)]
        return pltpu.make_async_remote_copy(
            src_ref=here, dst_ref=source.at[lines_of(s, core, b)],
            send_sem=ssem.at[n * SUB + b], recv_sem=rsem.at[n * SUB + b],
            device_id=(to * 2 + core, me_r), device_id_type=MESH,
        )

    def lift(n, b):
        return hop(n, b, chip - n, chip + 1, lift_ssem, lift_rsem)

    def sink(n, b):
        return hop(n, b, chip + n, chip - 1, sink_ssem, sink_rsem)

    def pass_on(s, b, own):
        here = x_hbm.at[pl.ds(b * step, step)] if own else source.at[lines_of(s, core, b)]
        return pltpu.make_async_remote_copy(
            src_ref=here, dst_ref=source.at[lines_of(s, core, b)],
            send_sem=share_ssem.at[s * SUB + b], recv_sem=share_rsem.at[s * SUB + b],
            device_id=(partner, me_r), device_id_type=MESH,
        )

    pl.semaphore_wait(barrier, dom_size + rep_size - 2)
    for b in range(SUB):

        @pl.when(chip < chips - 1)
        def _():
            lift(0, b).start()

        @pl.when(chip > 0)
        def _():
            sink(0, b).start()

    for b in range(SUB):
        pass_on(chip, b, True).start()

    def relay_source(n, b):
        @pl.when(chip - 1 - n >= 0)
        def _():
            lift(n, b).wait_recv()
            if n + 1 < chips - 1:

                @pl.when(chip < chips - 1)
                def _():
                    lift(n + 1, b).start()

            pass_on(chip - 1 - n, b, False).start()

        @pl.when(chip + 1 + n < chips)
        def _():
            sink(n, b).wait_recv()
            if n + 1 < chips - 1:

                @pl.when(chip > 0)
                def _():
                    sink(n + 1, b).start()

            pass_on(chip + 1 + n, b, False).start()

    small[0].wait()
    small[1].wait()
    order_tiles(count_ref[0], row_v[...], col_v[...], col_blocks, order_v, place_v, last_v)
    tables = [
        pltpu.make_async_copy(order_v, order, table_sem.at[0]),
        pltpu.make_async_copy(place_v, place, table_sem.at[1]),
        pltpu.make_async_copy(last_v, last, table_sem.at[2]),
    ]
    for copy in tables:
        copy.start()
    events = [(n, b) for n in range(chips - 1) for b in range(SUB)]
    relay_source(*events[0])
    scan[slots] = jnp.zeros((TILE, TILE), jnp.bfloat16)
    for copy in tables + loads + small[2:]:
        copy.wait()

    def merge(k, running):
        tile = raw[jnp.clip(order[0, k], 0, slots - 1)].astype(jnp.float32)
        more = place[0, k] == place[0, jnp.maximum(k - 1, 0)]
        running = jnp.where(more, running + tile, tile)
        scan[k] = running.astype(jnp.bfloat16)
        return running

    running = jnp.zeros((TILE, TILE), jnp.float32)
    early = [e for e in events[1:] if e[0] < chips - 2]
    spans = len(early) + 1
    ends = [slots * i // spans for i in range(spans + 1)]
    for i in range(spans):
        running = lax.fori_loop(ends[i], ends[i + 1], merge, running, unroll=2)
        if i < len(early):
            relay_source(*early[i])

    def at_place(spot):
        return scan[jnp.clip(last[0, spot], 0, slots)]

    def tile_rows(first, count, left, across):
        return jnp.concatenate(
            [
                jnp.concatenate(
                    [at_place((first + i) * col_blocks + left + j) for j in range(across)], axis=1
                )
                for i in range(count)
            ],
            axis=0,
        )

    def part_copy(t):
        return pltpu.make_async_remote_copy(
            src_ref=part_send.at[t], dst_ref=part_recv.at[t],
            send_sem=part_ssem.at[t], recv_sem=part_rsem.at[t],
            device_id=(me_d, rep_peer(t + 1)), device_id_type=MESH,
        )

    half = rows // 2

    def nearest(j):
        low = jnp.minimum(chip, chips - 1 - chip)
        n = (j - 1) // 2
        both = chip + (n + 1) * (2 * ((j - 1) % 2) - 1)
        up = jnp.where(chip < chips - 1 - chip, j, chips - 1 - j)
        return jnp.where(j <= 2 * low, both, up) if j else chip

    def forward(j):
        s = nearest(j)
        for b in range(SUB):
            pass_on(s, b, False).wait_recv()
        final = j == chips - 1

        def one(i, carry):
            t, h = i // 2, lax.rem(i, 2)
            ahead = rep_peer(t + 1)
            lines = pl.ds(pl.multiple_of(h * half, half), half)
            lanes = pl.ds(pl.multiple_of(h * width, width), width)
            left = tile_rows(ahead * blocks + h * (blocks // 2), blocks // 2, s * 2 * blocks, 2 * blocks)
            right = source[pl.ds(pl.multiple_of(s * 2 * rows, rows), 2 * rows), :]
            total = jnp.dot(left, right, preferred_element_type=jnp.float32)
            if j > 0:
                total = total + back[t, :, lanes]
            if not final:
                back[t, :, lanes] = total
                return carry

            @pl.when(t < rep_size - 1)
            def _():
                part_send[t, lines, :] = total.astype(jnp.bfloat16)

            @pl.when(t == rep_size - 1)
            def _():
                held[lines, :] = total

            @pl.when((t < rep_size - 1) & (h == 1))
            def _():
                part_copy(t).start()

            return carry

        lax.fori_loop(0, 2 * rep_size, one, 0)

    for j in range(chips):
        if j == chips - 1:
            for b in range(SUB):
                relay_source(chips - 2, b)
        forward(j)

    for t in range(rep_size - 1):
        part_copy(t).wait_recv()

    weight = weight_ref[...]

    def finish(h, carry):
        lines = pl.ds(pl.multiple_of(h * 128, 128), 128)
        total = held[lines, :]
        for t in range(rep_size - 1):
            total = total + part_recv[t, lines, :].astype(jnp.float32)
        high = total.astype(jnp.bfloat16)
        low = (total - high.astype(jnp.float32)).astype(jnp.bfloat16)
        summed = jnp.dot(high, weight, preferred_element_type=jnp.float32) + jnp.dot(
            low, weight, preferred_element_type=jnp.float32
        )
        sig = jax.nn.sigmoid(summed)
        out_ref[lines, :] = (summed * sig).astype(jnp.bfloat16)
        slope = sig * (1.0 + summed * (1.0 - sig))
        grad = (cot_ref[lines, :].astype(jnp.float32) * slope).astype(jnp.bfloat16)
        grads[0, lines, :] = grad
        held[lines, :] = total
        return carry

    lax.fori_loop(0, rows // 128, finish, 0)

    def grad_copy(u):
        return pltpu.make_async_remote_copy(
            src_ref=grads.at[0], dst_ref=grads.at[u],
            send_sem=grad_ssem.at[u], recv_sem=grad_rsem.at[u],
            device_id=(me_d, rep_peer(u)), device_id_type=MESH,
        )

    for u in range(1, rep_size):
        grad_copy(u).start()

    total = held[...]
    high = total.astype(jnp.bfloat16)
    low = (total - high.astype(jnp.float32)).astype(jnp.bfloat16)
    own_grad = grads[0]
    over_rows = (((0,), (0,)), ((), ()))
    own_term = lax.dot_general(high, own_grad, over_rows, preferred_element_type=jnp.float32)
    own_term = own_term + lax.dot_general(low, own_grad, over_rows, preferred_element_type=jnp.float32)
    gw2_send[...] = own_term
    gw1_send[...] = own_term.astype(jnp.bfloat16).reshape(dom_size, share, width)

    def gw1_copy(i):
        return pltpu.make_async_remote_copy(
            src_ref=gw1_send.at[dom_peer(i)], dst_ref=gw1_recv.at[i],
            send_sem=gw1_ssem.at[i], recv_sem=gw1_rsem.at[i],
            device_id=(dom_peer(i), me_r), device_id_type=MESH,
        )

    for i in range(1, dom_size):
        gw1_copy(i).start()

    def gw2_copy(i):
        return pltpu.make_async_remote_copy(
            src_ref=gw2_recv.at[me_r], dst_ref=gw2_recv.at[me_r],
            send_sem=gw2_ssem.at[i], recv_sem=gw2_rsem.at[i],
            device_id=(me_d, rep_peer(i)), device_id_type=MESH,
        )

    def gw3_copy(i):
        return pltpu.make_async_remote_copy(
            src_ref=gw3_recv.at[me_d], dst_ref=gw3_recv.at[me_d],
            send_sem=gw3_ssem.at[i], recv_sem=gw3_rsem.at[i],
            device_id=(dom_peer(i), me_r), device_id_type=MESH,
        )

    def weight_second():
        for i in range(1, dom_size):
            gw1_copy(i).wait_recv()
        mine = gw2_send[pl.ds(pl.multiple_of(me_d * share, share), share), :]
        for i in range(1, dom_size):
            mine = mine + gw1_recv[i].astype(jnp.float32)
        gw2_recv[me_r] = mine
        for i in range(1, rep_size):
            gw2_copy(i).start()

    def weight_third():
        for i in range(1, rep_size):
            gw2_copy(i).wait_recv()
        mine = gw2_recv[0]
        for i in range(1, rep_size):
            mine = mine + gw2_recv[i]
        gw3_recv[me_d] = mine.astype(jnp.bfloat16)
        for i in range(1, dom_size):
            gw3_copy(i).start()

    def back_step(u, flipped, group, d):
        right = tile_rows(group * blocks, blocks, d * blocks, blocks)
        product = jnp.dot(flipped, right, preferred_element_type=jnp.float32)

        @pl.when(u == 0)
        def _():
            back[d] = product

        @pl.when(u > 0)
        def _():
            back[d] = back[d] + product

    part = width // SPLIT

    def turn(j):
        odd = lax.rem(j, 2)
        return (1 - odd) * (chips - 1 - j // 2) + odd * (j // 2)

    def pair_copy(j):
        there = turn(j)
        return pltpu.make_async_remote_copy(
            src_ref=back.at[there * 2 + 1 - core], dst_ref=pair.at[there],
            send_sem=pair_ssem.at[j], recv_sem=pair_rsem.at[j],
            device_id=(partner, me_r), device_id_type=MESH,
        )

    def up_copy(q):
        return pltpu.make_async_remote_copy(
            src_ref=up_send.at[q], dst_ref=up_recv.at[q],
            send_sem=up_ssem.at[q], recv_sem=up_rsem.at[q],
            device_id=((chip + 1) * 2 + core, me_r), device_id_type=MESH,
        )

    def down_copy(q):
        return pltpu.make_async_remote_copy(
            src_ref=down_send.at[q], dst_ref=down_recv.at[q],
            send_sem=down_ssem.at[q], recv_sem=down_rsem.at[q],
            device_id=((chip - 1) * 2 + core, me_r), device_id_type=MESH,
        )

    def own_part(there, q):
        lines = pl.ds(pl.multiple_of(lax.rem(q, SPLIT) * part, part), part)
        return back[there * 2 + core, lines, :]

    def relay(tick):
        q_up = tick - chip
        q_down = tick - (chips - 1 - chip)

        @pl.when((chip > 0) & (q_up >= 0) & (q_up < SPLIT * (chips - 1 - chip)))
        def _():
            up_copy(q_up).wait_recv()
            up_send[q_up] = (
                own_part(chips - 1 - q_up // SPLIT, q_up) + up_recv[q_up].astype(jnp.float32)
            ).astype(jnp.bfloat16)
            up_copy(q_up).start()

        @pl.when((chip < chips - 1) & (q_down >= 0) & (q_down < SPLIT * chip))
        def _():
            down_copy(q_down).wait_recv()
            down_send[q_down] = (
                own_part(q_down // SPLIT, q_down) + down_recv[q_down].astype(jnp.float32)
            ).astype(jnp.bfloat16)
            down_copy(q_down).start()

    for u in range(rep_size):
        slot = rep_peer(rep_size - u)
        if u > 0:
            grad_copy(u).wait_recv()
        flipped = jnp.transpose(grads[u].astype(jnp.float32)).astype(jnp.bfloat16)
        if u < rep_size - 1:
            lax.fori_loop(0, dom_size, lambda d, c: (back_step(u, flipped, slot, d), c)[1], 0)
            if u == 1:
                weight_second()
            if u == 2:
                weight_third()
        else:

            def toward(j, carry):
                back_step(u, flipped, slot, turn(j) * 2 + 1 - core)
                pair_copy(j).start()
                return carry

            def keep(j, carry):
                there = turn(j)
                back_step(u, flipped, slot, there * 2 + core)
                pair_copy(j).wait_recv()
                back[there * 2 + core] = back[there * 2 + core] + pair[there]

                @pl.when((chip == 0) & (there > 0))
                def _():
                    for h in range(SPLIT):
                        q = (chips - 1 - there) * SPLIT + h
                        up_send[q] = own_part(there, q).astype(jnp.bfloat16)
                        up_copy(q).start()

                @pl.when((chip == chips - 1) & (there < chips - 1))
                def _():
                    for h in range(SPLIT):
                        q = there * SPLIT + h
                        down_send[q] = own_part(there, q).astype(jnp.bfloat16)
                        down_copy(q).start()

                return carry

            lax.fori_loop(0, chips, toward, 0)
            lax.fori_loop(0, chips, keep, 0)

    lax.fori_loop(1, SPLIT * (chips - 2) + 1, lambda tick, c: (relay(tick), c)[1], 0)

    for h in range(SPLIT):
        lines = pl.ds(h * part, part)

        @pl.when(chip > 0)
        def _():
            q = (chips - 1 - chip) * SPLIT + h
            up_copy(q).wait_recv()
            back[me_d, lines, :] = back[me_d, lines, :] + up_recv[q].astype(jnp.float32)

        @pl.when(chip < chips - 1)
        def _():
            q = chip * SPLIT + h
            down_copy(q).wait_recv()
            back[me_d, lines, :] = back[me_d, lines, :] + down_recv[q].astype(jnp.float32)

        gp_ref[lines, :] = back[me_d, lines, :].astype(jnp.bfloat16)

    for i in range(1, dom_size):
        gw3_copy(i).wait_recv()
    gw_ref[...] = gw3_recv[...].reshape(width, width)
    for t in range(rep_size - 1):
        part_copy(t).wait_send()
    for u in range(1, rep_size):
        grad_copy(u).wait_send()
        gw2_copy(u).wait_send()
    for i in range(1, dom_size):
        gw1_copy(i).wait_send()
        gw3_copy(i).wait_send()
    for j in range(chips):
        pair_copy(j).wait_send()

    def sent(q, carry):
        @pl.when((chip < chips - 1) & (q < SPLIT * (chips - 1 - chip)))
        def _():
            up_copy(q).wait_send()

        @pl.when((chip > 0) & (q < SPLIT * chip))
        def _():
            down_copy(q).wait_send()

        return carry

    lax.fori_loop(0, SPLIT * (chips - 1), sent, 0)

    for n in range(chips - 1):
        for b in range(SUB):

            @pl.when((chip < chips - 1) & (chip - n >= 0))
            def _():
                lift(n, b).wait_send()

            @pl.when((chip > 0) & (chip + n < chips))
            def _():
                sink(n, b).wait_send()

    for s in range(chips):
        for b in range(SUB):
            pass_on(s, b, False).wait_send()


def finish_kernel(raw_ref, gp_ref, gw_in_ref, weight_ref, out_ref, gf_ref, gw_ref):
    out_ref[...] = raw_ref[...]
    gw_ref[...] = gw_in_ref[...].astype(jnp.float32)
    grad_projected = jnp.transpose(gp_ref[...])
    gf_ref[...] = lax.dot_general(
        grad_projected, weight_ref[...], (((1,), (1,)), ((), ())), preferred_element_type=jnp.float32
    ).astype(jnp.bfloat16)


def finish(raw, grad_projected, grad_weight, weight):
    here = pl.BlockSpec(memory_space=pltpu.VMEM)
    return pl.pallas_call(
        finish_kernel,
        out_shape=(
            jax.ShapeDtypeStruct(raw.shape, jnp.bfloat16),
            jax.ShapeDtypeStruct(raw.shape, jnp.bfloat16),
            jax.ShapeDtypeStruct(grad_weight.shape, jnp.float32),
        ),
        in_specs=[here] * 4,
        out_specs=(here, here, here),
        name="finish",
        compiler_params=pltpu.CompilerParams(vmem_limit_bytes=16 * 2**20),
    )(raw, grad_projected, grad_weight, weight)


def room(scratch, extra):
    total = 0
    for item in scratch:
        if getattr(item, "memory_space", None) == pltpu.VMEM:
            size = jnp.dtype(item.dtype).itemsize
            for length in item.shape:
                size *= length
            total += size
    return total + extra


def run_layer(count, features, weight, cotangent, row_index, col_index, tiles, dom_size, rep_size):
    rows, width = cotangent.shape
    chips = dom_size // 2
    share = width // dom_size
    slots = tiles.shape[0]
    places = dom_size * rep_size * (rows // TILE) ** 2
    assert rows == 2 * width and rep_size <= dom_size
    here = pl.BlockSpec(memory_space=pltpu.VMEM)
    away = pl.BlockSpec(memory_space=pl.ANY)
    sems = lambda count: pltpu.SemaphoreType.DMA((count,))
    half, full, whole = jnp.bfloat16, jnp.float32, jnp.int32
    hops = SPLIT * (chips - 1)
    walks = SUB * (chips - 1)
    scratch = [
        pltpu.VMEM((dom_size * rows, width), half),
        pltpu.VMEM((slots, TILE, TILE), half),
        pltpu.VMEM((slots + 1, TILE, TILE), half),
        pltpu.VMEM((width, width), half),
        pltpu.VMEM((rows, width), half),
        pltpu.VMEM((1, slots), whole),
        pltpu.VMEM((1, slots), whole),
        pltpu.VMEM((1, slots), whole),
        pltpu.VMEM((1, slots), whole),
        pltpu.VMEM((1, places), whole),
        pltpu.SMEM((1, slots), whole),
        pltpu.SMEM((1, slots), whole),
        pltpu.SMEM((1, places), whole),
        pltpu.VMEM((rep_size - 1, rows, width), half),
        pltpu.VMEM((rep_size - 1, rows, width), half),
        pltpu.VMEM((rows, width), full),
        pltpu.VMEM((rep_size, rows, width), half),
        pltpu.VMEM((dom_size, width, rows), full),
        pltpu.VMEM((chips, width, rows), full),
        pltpu.VMEM((hops, width // SPLIT, rows), half),
        pltpu.VMEM((hops, width // SPLIT, rows), half),
        pltpu.VMEM((hops, width // SPLIT, rows), half),
        pltpu.VMEM((hops, width // SPLIT, rows), half),
        pltpu.VMEM((dom_size, share, width), half),
        pltpu.VMEM((dom_size, share, width), half),
        pltpu.VMEM((width, width), full),
        pltpu.VMEM((rep_size, share, width), full),
        pltpu.VMEM((dom_size, share, width), half),
        sems(LOADS), sems(5), sems(3), sems(walks), sems(walks), sems(walks), sems(walks),
        sems(SUB * chips), sems(SUB * chips),
        sems(rep_size), sems(rep_size), sems(rep_size), sems(rep_size),
        sems(chips), sems(chips), sems(hops), sems(hops), sems(hops), sems(hops),
        sems(dom_size), sems(dom_size), sems(rep_size), sems(rep_size),
        sems(dom_size), sems(dom_size),
    ]
    return pl.pallas_call(
        functools.partial(layer_kernel, dom_size, rep_size),
        out_shape=(
            jax.ShapeDtypeStruct((rows, width), half),
            jax.ShapeDtypeStruct((width, rows), half),
            jax.ShapeDtypeStruct((width, width), half),
        ),
        in_specs=[pl.BlockSpec(memory_space=pltpu.SMEM)] + [away] * 6,
        out_specs=(here, here, here),
        scratch_shapes=scratch,
        name="layer",
        compiler_params=pltpu.CompilerParams(
            collective_id=0, has_side_effects=True, vmem_limit_bytes=min(room(scratch, 6 * 2**20), 67043328)
        ),
    )(count, features, weight, cotangent, row_index, col_index, tiles)


def body(node_features, weight, cotangent, tile_row, tile_col, tile_values, tile_count):
    dom_size = lax.axis_size("dom")
    rep_size = lax.axis_size("rep")
    slots = tile_row.shape[2]
    raw, grad_projected, grad_weight = run_layer(
        tile_count.reshape(1),
        node_features,
        weight,
        cotangent,
        tile_row.reshape(1, slots),
        tile_col.reshape(1, slots),
        tile_values.reshape(slots, TILE, TILE),
        dom_size,
        rep_size,
    )
    return tuple(finish(raw, grad_projected, grad_weight, weight))


def solution(mesh):
    placed = (
        P(("dom", "rep"), None),
        P(),
        P(("dom", "rep"), None),
        P("dom", "rep", None),
        P("dom", "rep", None),
        P("dom", "rep", None, None, None),
        P("dom", "rep"),
    )
    return jax.shard_map(
        body,
        mesh=mesh,
        in_specs=placed,
        out_specs=(P(("dom", "rep"), None), P(("dom", "rep"), None), P()),
        check_vma=False,
    )
```

profile of v0, /device:TPU:9, one launch (start us, length us, event | category | flops | bytes accessed | tf_op | source)
XLA Modules:
  0.0 89.1 jit_solution(13341458868260116075)
XLA Ops:
  1.3 0.0 copy-start
  1.3 0.9 %copy-done = bf16[256,256]{1,0:T(8,128)(2,1)S(1)} copy-done((bf16[256,256]{1,0:T(8,128)(2,1)S(1)}, bf16[256,256]{1,0:T(8,128)(2,1)}, u32[]{:S(2)}) %copy-start) | copy-done | bytes 131096
  2.2 0.0 copy-start.1
  2.2 0.7 copy-done.1
  2.9 0.0 copy-start.2
  2.9 0.7 copy-done.2
  3.5 84.5 %layer.1 = (bf16[512,256]{1,0:T(8,128)(2,1)S(1)}, bf16[256,512]{1,0:T(8,128)(2,1)S(1)}, bf16[256,256]{1,0:T(8,128)(2,1)S(1)}) custom-call(s32[1]{0:T(128)} %bitcast.4.refs_0_, bf16[512,256]{1,0:T(8,128)(2,1)} %refs_1_.1, bf16[256,256]{1,0:T(8,128)(2,1)S(1)} %copy-done, bf16[512,256]{1,0:T(8,128)(2,1)} %refs_3_.1, s32[1,512]{1,0:T(1,128)S(1)} %bitcast.5, ...), custom_call_target="tpu_custom_call" | custom-call | tf_op jit(solution)/shard_map/layer/pallas_call | solution.py:625
  88.0 1.1 %finish.1 = (bf16[512,256]{1,0:T(8,128)(2,1)}, bf16[512,256]{1,0:T(8,128)(2,1)}, f32[256,256]{1,0:T(8,128)}) custom-call(bf16[512,256]{1,0:T(8,128)(2,1)S(1)} %get-tuple-element.6.raw_ref, bf16[256,512]{1,0:T(8,128)(2,1)S(1)} %get-tuple-element.7.gp_ref, bf16[256,256]{1,0:T(8,128)(2,1)S(1)} %get-tuple-element.8.gw_in_ref, bf16[256,256]{1,0:T(8,128)(2,1)S(1)} %copy-done), custom_call_target="tpu_custom_call" | custom-call | tf_op jit(solution)/shard_map/finish/pallas_call | solution.py:551
Async XLA Ops:
  1.3 0.9 %copy-start = (bf16[256,256]{1,0:T(8,128)(2,1)S(1)}, bf16[256,256]{1,0:T(8,128)(2,1)}, u32[]{:S(2)}) copy-start(bf16[256,256]{1,0:T(8,128)(2,1)} %weight_ref.1) | copy-start | bytes 393220
  2.2 0.7 copy-start.1
  2.9 0.7 copy-start.2
where the time goes:
time: 89.3 us; the launch traced here: 89.1 us
  Pallas kernels  85.5 us (96%)
  local copies, waits for them, and re-layouts  2.26 us (3%)
  between operations  1.3 us (1%)
    pallas_call x1, Pallas kernels, run_layer(): pl.pallas_call(functools.partial(layer_kernel, dom_size, rep_size), out_s...  84.5 us
    unnamed x6, local copies, waits for them, and re-layouts  2.26 us

commit v1 on v0

--- a/solution.py
+++ b/solution.py
@@ -10,6 +10,7 @@
 LOADS = 8
 SUB = 2
 SPLIT = 4
+HALVES = 2
 TILE = 128
 MESH = pl.DeviceIdType.MESH
 
@@ -63,10 +64,10 @@
     (
         count_ref, x_hbm, weight_hbm, cot_hbm, row_hbm, col_hbm, tiles_hbm, out_ref, gp_ref, gw_ref,
         source, raw, scan, weight_ref, cot_ref, row_v, col_v, order_v, place_v, last_v, order, place, last,
-        part_send, part_recv, held, grads, back, pair, up_send, up_recv, down_send, down_recv,
+        near_send, near_recv, far_send, far_recv, held, grads, back, pair, up_send, up_recv, down_send, down_recv,
         gw1_send, gw1_recv, gw2_send, gw2_recv, gw3_recv,
         raw_sem, small_sem, table_sem, lift_ssem, lift_rsem, sink_ssem, sink_rsem, share_ssem, share_rsem,
-        part_ssem, part_rsem, grad_ssem, grad_rsem, pair_ssem, pair_rsem, up_ssem, up_rsem, down_ssem, down_rsem,
+        near_ssem, near_rsem, far_ssem, far_rsem, grad_ssem, grad_rsem, pair_ssem, pair_rsem, up_ssem, up_rsem, down_ssem, down_rsem,
         gw1_ssem, gw1_rsem, gw2_ssem, gw2_rsem, gw3_ssem, gw3_rsem,
     ) = refs
     rows, width = cot_ref.shape
@@ -190,6 +191,8 @@
     scan[slots] = jnp.zeros((TILE, TILE), jnp.bfloat16)
     for copy in tables + loads + small[2:]:
         copy.wait()
+    if len(events) > 1:
+        relay_source(*events[1])
 
     def merge(k, running):
         tile = raw[jnp.clip(order[0, k], 0, slots - 1)].astype(jnp.float32)
@@ -199,8 +202,8 @@
         return running
 
     running = jnp.zeros((TILE, TILE), jnp.float32)
-    early = [e for e in events[1:] if e[0] < chips - 2]
-    spans = len(early) + 1
+    early = [e for e in events[2:] if e[0] < chips - 2]
+    spans = max(len(early), 1)
     ends = [slots * i // spans for i in range(spans + 1)]
     for i in range(spans):
         running = lax.fori_loop(ends[i], ends[i + 1], merge, running, unroll=2)
@@ -221,11 +224,24 @@
             axis=0,
         )
 
-    def part_copy(t):
-        return pltpu.make_async_remote_copy(
-            src_ref=part_send.at[t], dst_ref=part_recv.at[t],
-            send_sem=part_ssem.at[t], recv_sem=part_rsem.at[t],
-            device_id=(me_d, rep_peer(t + 1)), device_id_type=MESH,
+    outer_size = rep_size // 2
+    outer, inner = me_r // 2, lax.rem(me_r, 2)
+
+    def outer_peer(i):
+        return lax.rem(outer + i, outer_size)
+
+    def near_copy(i):
+        return pltpu.make_async_remote_copy(
+            src_ref=near_send.at[i], dst_ref=near_recv.at[i],
+            send_sem=near_ssem.at[i], recv_sem=near_rsem.at[i],
+            device_id=(me_d, outer * 2 + 1 - inner), device_id_type=MESH,
+        )
+
+    def far_copy(i, k):
+        return pltpu.make_async_remote_copy(
+            src_ref=far_send.at[i - 1, k], dst_ref=far_recv.at[i - 1, k],
+            send_sem=far_ssem.at[(i - 1) * 3 + k], recv_sem=far_rsem.at[(i - 1) * 3 + k],
+            device_id=(me_d, outer_peer(i) * 2 + inner), device_id_type=MESH,
         )
 
     half = rows // 2
@@ -243,35 +259,36 @@
             pass_on(s, b, False).wait_recv()
         final = j == chips - 1
 
-        def one(i, carry):
-            t, h = i // 2, lax.rem(i, 2)
-            ahead = rep_peer(t + 1)
-            lines = pl.ds(pl.multiple_of(h * half, half), half)
-            lanes = pl.ds(pl.multiple_of(h * width, width), width)
-            left = tile_rows(ahead * blocks + h * (blocks // 2), blocks // 2, s * 2 * blocks, 2 * blocks)
+        def one(t, carry):
+            i = lax.rem(t // 2 + 1, outer_size)
+            side = lax.rem(t, 2)
+            ahead = outer_peer(i) * 2 + (1 - side) * (1 - inner) + side * inner
+            left = tile_rows(ahead * blocks, blocks, s * 2 * blocks, 2 * blocks)
             right = source[pl.ds(pl.multiple_of(s * 2 * rows, rows), 2 * rows), :]
             total = jnp.dot(left, right, preferred_element_type=jnp.float32)
             if j > 0:
-                total = total + back[t, :, lanes]
+                total = total + jnp.concatenate([back[t, :, :width], back[t, :, width:]], axis=0)
             if not final:
-                back[t, :, lanes] = total
+                back[t, :, :width] = total[:half]
+                back[t, :, width:] = total[half:]
                 return carry
 
-            @pl.when(t < rep_size - 1)
-            def _():
-                part_send[t, lines, :] = total.astype(jnp.bfloat16)
-
-            @pl.when(t == rep_size - 1)
-            def _():
-                held[lines, :] = total
-
-            @pl.when((t < rep_size - 1) & (h == 1))
-            def _():
-                part_copy(t).start()
+            back[t, :, :width] = total[:half]
+            back[t, :, width:] = total[half:]
+
+            @pl.when(side == 0)
+            def _():
+                near_send[i] = total[:half].astype(jnp.bfloat16)
+                near_copy(i).start()
+
+            @pl.when(i > 0)
+            def _():
+                far_send[i - 1, side] = total[half:].astype(jnp.bfloat16)
+                far_copy(i, side).start()
 
             return carry
 
-        lax.fori_loop(0, 2 * rep_size, one, 0)
+        lax.fori_loop(0, rep_size, one, 0)
 
     for j in range(chips):
         if j == chips - 1:
@@ -279,16 +296,42 @@
                 relay_source(chips - 2, b)
         forward(j)
 
-    for t in range(rep_size - 1):
-        part_copy(t).wait_recv()
+    for i in range(1, outer_size):
+        near_copy(i).wait_recv()
+        far_send[i - 1, 2] = (
+            back[2 * i - 1, :, :width] + near_recv[i].astype(jnp.float32)
+        ).astype(jnp.bfloat16)
+        far_copy(i, 2).start()
+    for i in range(1, outer_size):
+        far_copy(i, 0).wait_recv()
+    beside = back[rep_size - 2, :, width:]
+    for i in range(1, outer_size):
+        beside = beside + far_recv[i - 1, 0].astype(jnp.float32)
+    near_send[outer_size] = beside.astype(jnp.bfloat16)
+    near_copy(outer_size).start()
+    near_copy(0).wait_recv()
+    upper = back[rep_size - 1, :, :width] + near_recv[0].astype(jnp.float32)
+    lower = back[rep_size - 1, :, width:]
+    for i in range(1, outer_size):
+        far_copy(i, 1).wait_recv()
+        lower = lower + far_recv[i - 1, 1].astype(jnp.float32)
+    held[:half, :] = upper
+    held[half:, :] = lower
+    for i in range(1, outer_size):
+        far_copy(i, 2).wait_recv()
+    near_copy(outer_size).wait_recv()
 
     weight = weight_ref[...]
+    slab = width // HALVES
 
     def finish(h, carry):
         lines = pl.ds(pl.multiple_of(h * 128, 128), 128)
         total = held[lines, :]
-        for t in range(rep_size - 1):
-            total = total + part_recv[t, lines, :].astype(jnp.float32)
+        piece = pl.ds(pl.multiple_of(lax.rem(h, half // 128) * 128, 128), 128)
+        late = far_recv[0, 2, piece, :].astype(jnp.float32)
+        for i in range(2, outer_size):
+            late = late + far_recv[i - 1, 2, piece, :].astype(jnp.float32)
+        total = total + jnp.where(h < half // 128, late, near_recv[outer_size, piece, :].astype(jnp.float32))
         high = total.astype(jnp.bfloat16)
         low = (total - high.astype(jnp.float32)).astype(jnp.bfloat16)
         summed = jnp.dot(high, weight, preferred_element_type=jnp.float32) + jnp.dot(
@@ -298,26 +341,27 @@
         out_ref[lines, :] = (summed * sig).astype(jnp.bfloat16)
         slope = sig * (1.0 + summed * (1.0 - sig))
         grad = (cot_ref[lines, :].astype(jnp.float32) * slope).astype(jnp.bfloat16)
-        grads[0, lines, :] = grad
+        for h in range(HALVES):
+            grads[h, 0, lines, :] = grad[:, h * slab : (h + 1) * slab]
         held[lines, :] = total
         return carry
 
     lax.fori_loop(0, rows // 128, finish, 0)
 
-    def grad_copy(u):
-        return pltpu.make_async_remote_copy(
-            src_ref=grads.at[0], dst_ref=grads.at[u],
-            send_sem=grad_ssem.at[u], recv_sem=grad_rsem.at[u],
+    def grad_copy(u, h):
+        return pltpu.make_async_remote_copy(
+            src_ref=grads.at[h, 0], dst_ref=grads.at[h, u],
+            send_sem=grad_ssem.at[h * rep_size + u], recv_sem=grad_rsem.at[h * rep_size + u],
             device_id=(me_d, rep_peer(u)), device_id_type=MESH,
         )
 
     for u in range(1, rep_size):
-        grad_copy(u).start()
+        grad_copy(u, 0).start()
 
     total = held[...]
     high = total.astype(jnp.bfloat16)
     low = (total - high.astype(jnp.float32)).astype(jnp.bfloat16)
-    own_grad = grads[0]
+    own_grad = jnp.concatenate([grads[h, 0] for h in range(HALVES)], axis=1)
     over_rows = (((0,), (0,)), ((), ()))
     own_term = lax.dot_general(high, own_grad, over_rows, preferred_element_type=jnp.float32)
     own_term = own_term + lax.dot_general(low, own_grad, over_rows, preferred_element_type=jnp.float32)
@@ -368,158 +412,187 @@
         for i in range(1, dom_size):
             gw3_copy(i).start()
 
-    def back_step(u, flipped, group, d):
-        right = tile_rows(group * blocks, blocks, d * blocks, blocks)
+    part = width // SPLIT
+    each = SPLIT // HALVES
+    hops = each * (chips - 1)
+
+    def slab_of(h):
+        return pl.ds(h * slab, slab)
+
+    def back_step(u, h, flipped, d):
+        right = tile_rows(rep_peer(rep_size - u) * blocks, blocks, d * blocks, blocks)
         product = jnp.dot(flipped, right, preferred_element_type=jnp.float32)
-
-        @pl.when(u == 0)
-        def _():
-            back[d] = product
-
-        @pl.when(u > 0)
-        def _():
-            back[d] = back[d] + product
-
-    part = width // SPLIT
+        if u > 0:
+            product = back[d, slab_of(h), :] + product
+        back[d, slab_of(h), :] = product
+
+    def flip(u, h):
+        return jnp.transpose(grads[h, u].astype(jnp.float32)).astype(jnp.bfloat16)
+
+    def back_all(u, h):
+        if u > 0:
+            grad_copy(u, h).wait_recv()
+        flipped = flip(u, h)
+        lax.fori_loop(0, dom_size, lambda d, c: (back_step(u, h, flipped, d), c)[1], 0)
 
     def turn(j):
         odd = lax.rem(j, 2)
         return (1 - odd) * (chips - 1 - j // 2) + odd * (j // 2)
 
-    def pair_copy(j):
+    def pair_copy(j, h):
         there = turn(j)
         return pltpu.make_async_remote_copy(
-            src_ref=back.at[there * 2 + 1 - core], dst_ref=pair.at[there],
-            send_sem=pair_ssem.at[j], recv_sem=pair_rsem.at[j],
+            src_ref=back.at[there * 2 + 1 - core, slab_of(h)], dst_ref=pair.at[there, slab_of(h)],
+            send_sem=pair_ssem.at[h * chips + j], recv_sem=pair_rsem.at[h * chips + j],
             device_id=(partner, me_r), device_id_type=MESH,
         )
 
-    def up_copy(q):
-        return pltpu.make_async_remote_copy(
-            src_ref=up_send.at[q], dst_ref=up_recv.at[q],
-            send_sem=up_ssem.at[q], recv_sem=up_rsem.at[q],
+    def up_copy(q, h):
+        return pltpu.make_async_remote_copy(
+            src_ref=up_send.at[h * hops + q], dst_ref=up_recv.at[h * hops + q],
+            send_sem=up_ssem.at[h * hops + q], recv_sem=up_rsem.at[h * hops + q],
             device_id=((chip + 1) * 2 + core, me_r), device_id_type=MESH,
         )
 
-    def down_copy(q):
-        return pltpu.make_async_remote_copy(
-            src_ref=down_send.at[q], dst_ref=down_recv.at[q],
-            send_sem=down_ssem.at[q], recv_sem=down_rsem.at[q],
+    def down_copy(q, h):
+        return pltpu.make_async_remote_copy(
+            src_ref=down_send.at[h * hops + q], dst_ref=down_recv.at[h * hops + q],
+            send_sem=down_ssem.at[h * hops + q], recv_sem=down_rsem.at[h * hops + q],
             device_id=((chip - 1) * 2 + core, me_r), device_id_type=MESH,
         )
 
-    def own_part(there, q):
-        lines = pl.ds(pl.multiple_of(lax.rem(q, SPLIT) * part, part), part)
+    def own_part(there, q, h):
+        lines = pl.ds(pl.multiple_of(h * slab + lax.rem(q, each) * part, part), part)
         return back[there * 2 + core, lines, :]
 
-    def relay(tick):
+    def relay(tick, h):
         q_up = tick - chip
         q_down = tick - (chips - 1 - chip)
 
-        @pl.when((chip > 0) & (q_up >= 0) & (q_up < SPLIT * (chips - 1 - chip)))
+        @pl.when((chip > 0) & (q_up >= 0) & (q_up < each * (chips - 1 - chip)))
         def _():
-            up_copy(q_up).wait_recv()
-            up_send[q_up] = (
-                own_part(chips - 1 - q_up // SPLIT, q_up) + up_recv[q_up].astype(jnp.float32)
+            up_copy(q_up, h).wait_recv()
+            up_send[h * hops + q_up] = (
+                own_part(chips - 1 - q_up // each, q_up, h) + up_recv[h * hops + q_up].astype(jnp.float32)
             ).astype(jnp.bfloat16)
-            up_copy(q_up).start()
-
-        @pl.when((chip < chips - 1) & (q_down >= 0) & (q_down < SPLIT * chip))
+            up_copy(q_up, h).start()
+
+        @pl.when((chip < chips - 1) & (q_down >= 0) & (q_down < each * chip))
         def _():
-            down_copy(q_down).wait_recv()
-            down_send[q_down] = (
-                own_part(q_down // SPLIT, q_down) + down_recv[q_down].astype(jnp.float32)
+            down_copy(q_down, h).wait_recv()
+            down_send[h * hops + q_down] = (
+                own_part(q_down // each, q_down, h) + down_recv[h * hops + q_down].astype(jnp.float32)
             ).astype(jnp.bfloat16)
-            down_copy(q_down).start()
-
-    for u in range(rep_size):
-        slot = rep_peer(rep_size - u)
-        if u > 0:
-            grad_copy(u).wait_recv()
-        flipped = jnp.transpose(grads[u].astype(jnp.float32)).astype(jnp.bfloat16)
-        if u < rep_size - 1:
-            lax.fori_loop(0, dom_size, lambda d, c: (back_step(u, flipped, slot, d), c)[1], 0)
-            if u == 1:
-                weight_second()
-            if u == 2:
-                weight_third()
-        else:
-
-            def toward(j, carry):
-                back_step(u, flipped, slot, turn(j) * 2 + 1 - core)
-                pair_copy(j).start()
-                return carry
-
-            def keep(j, carry):
-                there = turn(j)
-                back_step(u, flipped, slot, there * 2 + core)
-                pair_copy(j).wait_recv()
-                back[there * 2 + core] = back[there * 2 + core] + pair[there]
-
-                @pl.when((chip == 0) & (there > 0))
-                def _():
-                    for h in range(SPLIT):
-                        q = (chips - 1 - there) * SPLIT + h
-                        up_send[q] = own_part(there, q).astype(jnp.bfloat16)
-                        up_copy(q).start()
-
-                @pl.when((chip == chips - 1) & (there < chips - 1))
-                def _():
-                    for h in range(SPLIT):
-                        q = there * SPLIT + h
-                        down_send[q] = own_part(there, q).astype(jnp.bfloat16)
-                        down_copy(q).start()
-
-                return carry
-
-            lax.fori_loop(0, chips, toward, 0)
-            lax.fori_loop(0, chips, keep, 0)
-
-    lax.fori_loop(1, SPLIT * (chips - 2) + 1, lambda tick, c: (relay(tick), c)[1], 0)
-
-    for h in range(SPLIT):
-        lines = pl.ds(h * part, part)
-
-        @pl.when(chip > 0)
-        def _():
-            q = (chips - 1 - chip) * SPLIT + h
-            up_copy(q).wait_recv()
-            back[me_d, lines, :] = back[me_d, lines, :] + up_recv[q].astype(jnp.float32)
-
-        @pl.when(chip < chips - 1)
-        def _():
-            q = chip * SPLIT + h
-            down_copy(q).wait_recv()
-            back[me_d, lines, :] = back[me_d, lines, :] + down_recv[q].astype(jnp.float32)
-
-        gp_ref[lines, :] = back[me_d, lines, :].astype(jnp.bfloat16)
+            down_copy(q_down, h).start()
+
+    def relays(first, after, h):
+        lax.fori_loop(first, after, lambda tick, c: (relay(tick, h), c)[1], 0)
+
+    def back_last(h, between):
+        u = rep_size - 1
+        grad_copy(u, h).wait_recv()
+        flipped = flip(u, h)
+
+        def toward(j, carry):
+            back_step(u, h, flipped, turn(j) * 2 + 1 - core)
+            pair_copy(j, h).start()
+            return carry
+
+        def keep(j, carry):
+            there = turn(j)
+            back_step(u, h, flipped, there * 2 + core)
+            pair_copy(j, h).wait_recv()
+            mine = there * 2 + core
+            back[mine, slab_of(h), :] = back[mine, slab_of(h), :] + pair[there, slab_of(h), :]
+
+            @pl.when((chip == 0) & (there > 0))
+            def _():
+                for i in range(each):
+                    q = (chips - 1 - there) * each + i
+                    up_send[h * hops + q] = own_part(there, q, h).astype(jnp.bfloat16)
+                    up_copy(q, h).start()
+
+            @pl.when((chip == chips - 1) & (there < chips - 1))
+            def _():
+                for i in range(each):
+                    q = there * each + i
+                    down_send[h * hops + q] = own_part(there, q, h).astype(jnp.bfloat16)
+                    down_copy(q, h).start()
+
+            return carry
+
+        lax.fori_loop(0, chips, toward, 0)
+        between()
+        lax.fori_loop(0, chips, keep, 0)
+
+    ticks = each * (chips - 2)
+    for h in range(HALVES):
+        back_all(0, h)
+    weight_second()
+    for h in range(1, HALVES):
+        for u in range(1, rep_size):
+            grad_copy(u, h).start()
+    for u in range(1, rep_size - 1):
+        back_all(u, 0)
+    back_last(0, weight_third)
+    for h in range(1, HALVES):
+        for u in range(1, rep_size - 1):
+            back_all(u, h)
+            relays(1 + ticks * (u - 1) // (rep_size - 1), 1 + ticks * u // (rep_size - 1), h - 1)
+        back_last(h, lambda: relays(1 + ticks * (rep_size - 2) // (rep_size - 1), 1 + ticks, h - 1))
+    relays(1, 1 + ticks, HALVES - 1)
+
+    for h in range(HALVES):
+        for i in range(each):
+            lines = pl.ds(h * slab + i * part, part)
+
+            @pl.when(chip > 0)
+            def _():
+                q = (chips - 1 - chip) * each + i
+                up_copy(q, h).wait_recv()
+                back[me_d, lines, :] = back[me_d, lines, :] + up_recv[h * hops + q].astype(jnp.float32)
+
+            @pl.when(chip < chips - 1)
+            def _():
+                q = chip * each + i
+                down_copy(q, h).wait_recv()
+                back[me_d, lines, :] = back[me_d, lines, :] + down_recv[h * hops + q].astype(jnp.float32)
+
+            gp_ref[lines, :] = back[me_d, lines, :].astype(jnp.bfloat16)
 
     for i in range(1, dom_size):
         gw3_copy(i).wait_recv()
     gw_ref[...] = gw3_recv[...].reshape(width, width)
-    for t in range(rep_size - 1):
-        part_copy(t).wait_send()
+    for i in range(outer_size + 1):
+        near_copy(i).wait_send()
+    for i in range(1, outer_size):
+        for k in range(3):
+            far_copy(i, k).wait_send()
     for u in range(1, rep_size):
-        grad_copy(u).wait_send()
+        for h in range(HALVES):
+            grad_copy(u, h).wait_send()
         gw2_copy(u).wait_send()
     for i in range(1, dom_size):
         gw1_copy(i).wait_send()
         gw3_copy(i).wait_send()
     for j in range(chips):
-        pair_copy(j).wait_send()
+        for h in range(HALVES):
+            pair_copy(j, h).wait_send()
 
     def sent(q, carry):
-        @pl.when((chip < chips - 1) & (q < SPLIT * (chips - 1 - chip)))
-        def _():
-            up_copy(q).wait_send()
-
-        @pl.when((chip > 0) & (q < SPLIT * chip))
-        def _():
-            down_copy(q).wait_send()
+        for h in range(HALVES):
+
+            @pl.when((chip < chips - 1) & (q < each * (chips - 1 - chip)))
+            def _():
+                up_copy(q, h).wait_send()
+
+            @pl.when((chip > 0) & (q < each * chip))
+            def _():
+                down_copy(q, h).wait_send()
 
         return carry
 
-    lax.fori_loop(0, SPLIT * (chips - 1), sent, 0)
+    lax.fori_loop(0, hops, sent, 0)
 
     for n in range(chips - 1):
         for b in range(SUB):
@@ -581,7 +654,7 @@
     places = dom_size * rep_size * (rows // TILE) ** 2
     assert rows == 2 * width and rep_size <= dom_size
     here = pl.BlockSpec(memory_space=pltpu.VMEM)
-    away = pl.BlockSpec(memory_space=pl.ANY)
+    away = pl.BlockSpec(memory_space=pltpu.HBM)
     sems = lambda count: pltpu.SemaphoreType.DMA((count,))
     half, full, whole = jnp.bfloat16, jnp.float32, jnp.int32
     hops = SPLIT * (chips - 1)
@@ -600,10 +673,12 @@
         pltpu.SMEM((1, slots), whole),
         pltpu.SMEM((1, slots), whole),
         pltpu.SMEM((1, places), whole),
-        pltpu.VMEM((rep_size - 1, rows, width), half),
-        pltpu.VMEM((rep_size - 1, rows, width), half),
+        pltpu.VMEM((rep_size // 2 + 1, rows // 2, width), half),
+        pltpu.VMEM((rep_size // 2 + 1, rows // 2, width), half),
+        pltpu.VMEM((rep_size // 2 - 1, 3, rows // 2, width), half),
+        pltpu.VMEM((rep_size // 2 - 1, 3, rows // 2, width), half),
         pltpu.VMEM((rows, width), full),
-        pltpu.VMEM((rep_size, rows, width), half),
+        pltpu.VMEM((HALVES, rep_size, rows, width // HALVES), half),
         pltpu.VMEM((dom_size, width, rows), full),
         pltpu.VMEM((chips, width, rows), full),
         pltpu.VMEM((hops, width // SPLIT, rows), half),
@@ -617,8 +692,9 @@
         pltpu.VMEM((dom_size, share, width), half),
         sems(LOADS), sems(5), sems(3), sems(walks), sems(walks), sems(walks), sems(walks),
         sems(SUB * chips), sems(SUB * chips),
-        sems(rep_size), sems(rep_size), sems(rep_size), sems(rep_size),
-        sems(chips), sems(chips), sems(hops), sems(hops), sems(hops), sems(hops),
+        sems(rep_size // 2 + 1), sems(rep_size // 2 + 1), sems(3 * (rep_size // 2 - 1)), sems(3 * (rep_size // 2 - 1)),
+        sems(HALVES * rep_size), sems(HALVES * rep_size),
+        sems(HALVES * chips), sems(HALVES * chips), sems(hops), sems(hops), sems(hops), sems(hops),
         sems(dom_size), sems(dom_size), sems(rep_size), sems(rep_size),
         sems(dom_size), sems(dom_size),
     ]

time: 89.3 us -> 80.2 us (0.90)
  the two profiles are of different devices: /device:TPU:9 before, /device:TPU:0 now
where the time goes in v1:
time: 80.2 us; the launch traced here: 80 us
  Pallas kernels  76.5 us (95%)
  local copies, waits for them, and re-layouts  2.26 us (3%)
  between operations  1.3 us (2%)
    pallas_call x1, Pallas kernels, run_layer(): pl.pallas_call(functools.partial(layer_kernel, dom_size, rep_size), out_s...  75.4 us
    unnamed x6, local copies, waits for them, and re-layouts  2.26 us

profile of v1, /device:TPU:0, one launch (start us, length us, event | category | flops | bytes accessed | tf_op | source)
XLA Modules:
  0.0 80.0 jit_solution(2414540506745193089)
XLA Ops:
  1.3 0.0 copy-start
  1.3 0.9 %copy-done = bf16[256,256]{1,0:T(8,128)(2,1)S(1)} copy-done((bf16[256,256]{1,0:T(8,128)(2,1)S(1)}, bf16[256,256]{1,0:T(8,128)(2,1)}, u32[]{:S(2)}) %copy-start) | copy-done | bytes 131096
  2.2 0.0 copy-start.1
  2.2 0.7 copy-done.1
  2.9 0.0 copy-start.2
  2.9 0.7 copy-done.2
  3.5 75.4 %layer.1 = (bf16[512,256]{1,0:T(8,128)(2,1)S(1)}, bf16[256,512]{1,0:T(8,128)(2,1)S(1)}, bf16[256,256]{1,0:T(8,128)(2,1)S(1)}) custom-call(s32[1]{0:T(128)} %bitcast.4.refs_0_, bf16[512,256]{1,0:T(8,128)(2,1)} %refs_1_.1, bf16[256,256]{1,0:T(8,128)(2,1)S(1)} %copy-done, bf16[512,256]{1,0:T(8,128)(2,1)} %refs_3_.1, s32[1,512]{1,0:T(1,128)S(1)} %bitcast.5, ...), custom_call_target="tpu_custom_call" | custom-call | tf_op jit(solution)/shard_map/layer/pallas_call | solution.py:701
  79.0 1.1 %finish.1 = (bf16[512,256]{1,0:T(8,128)(2,1)}, bf16[512,256]{1,0:T(8,128)(2,1)}, f32[256,256]{1,0:T(8,128)}) custom-call(bf16[512,256]{1,0:T(8,128)(2,1)S(1)} %get-tuple-element.6.raw_ref, bf16[256,512]{1,0:T(8,128)(2,1)S(1)} %get-tuple-element.7.gp_ref, bf16[256,256]{1,0:T(8,128)(2,1)S(1)} %get-tuple-element.8.gw_in_ref, bf16[256,256]{1,0:T(8,128)(2,1)S(1)} %copy-done), custom_call_target="tpu_custom_call" | custom-call | tf_op jit(solution)/shard_map/finish/pallas_call | solution.py:624
Async XLA Ops:
  1.3 0.9 %copy-start = (bf16[256,256]{1,0:T(8,128)(2,1)S(1)}, bf16[256,256]{1,0:T(8,128)(2,1)}, u32[]{:S(2)}) copy-start(bf16[256,256]{1,0:T(8,128)(2,1)} %weight_ref.1) | copy-start | bytes 393220
  2.2 0.7 copy-start.1
  2.9 0.7 copy-start.2

commit v2 on v1

--- a/solution.py
+++ b/solution.py
@@ -9,7 +9,7 @@
 
 LOADS = 8
 SUB = 2
-SPLIT = 4
+SPLIT = 2
 HALVES = 2
 TILE = 128
 MESH = pl.DeviceIdType.MESH
@@ -67,7 +67,7 @@
         near_send, near_recv, far_send, far_recv, held, grads, back, pair, up_send, up_recv, down_send, down_recv,
         gw1_send, gw1_recv, gw2_send, gw2_recv, gw3_recv,
         raw_sem, small_sem, table_sem, lift_ssem, lift_rsem, sink_ssem, sink_rsem, share_ssem, share_rsem,
-        near_ssem, near_rsem, far_ssem, far_rsem, grad_ssem, grad_rsem, pair_ssem, pair_rsem, up_ssem, up_rsem, down_ssem, down_rsem,
+        near_ssem, near_rsem, far_ssem, far_rsem, near_gsend, near_grecv, far_gsend, far_grecv, pair_ssem, pair_rsem, up_ssem, up_rsem, down_ssem, down_rsem,
         gw1_ssem, gw1_rsem, gw2_ssem, gw2_rsem, gw3_ssem, gw3_rsem,
     ) = refs
     rows, width = cot_ref.shape
@@ -348,15 +348,50 @@
 
     lax.fori_loop(0, rows // 128, finish, 0)
 
-    def grad_copy(u, h):
-        return pltpu.make_async_remote_copy(
-            src_ref=grads.at[h, 0], dst_ref=grads.at[h, u],
-            send_sem=grad_ssem.at[h * rep_size + u], recv_sem=grad_rsem.at[h * rep_size + u],
-            device_id=(me_d, rep_peer(u)), device_id_type=MESH,
-        )
-
-    for u in range(1, rep_size):
-        grad_copy(u, 0).start()
+    def row_half(p):
+        return pl.ds(p * half, half)
+
+    def near_grad(h, i, p):
+        k = h * (outer_size + 1) + (p if i == 0 else 1 + i)
+        return pltpu.make_async_remote_copy(
+            src_ref=grads.at[h, 2 * i, row_half(p)], dst_ref=grads.at[h, 2 * i + 1, row_half(p)],
+            send_sem=near_gsend.at[k], recv_sem=near_grecv.at[k],
+            device_id=(me_d, outer * 2 + 1 - inner), device_id_type=MESH,
+        )
+
+    def far_grad(h, i, side, p):
+        k = (h * (outer_size - 1) + i - 1) * 3 + (2 if side else p)
+        return pltpu.make_async_remote_copy(
+            src_ref=grads.at[h, side, row_half(p)], dst_ref=grads.at[h, 2 * i + side, row_half(p)],
+            send_sem=far_gsend.at[k], recv_sem=far_grecv.at[k],
+            device_id=(me_d, outer_peer(i) * 2 + inner), device_id_type=MESH,
+        )
+
+    def spread_grads(h):
+        for p in range(2):
+            near_grad(h, 0, p).start()
+            for i in range(1, outer_size):
+                far_grad(h, i, 0, 1 - p).start()
+
+    def relay_grads(h):
+        near_grad(h, 0, 0).wait_recv()
+        for i in range(1, outer_size):
+            far_grad(h, i, 1, 0).start()
+        for i in range(1, outer_size):
+            far_grad(h, i, 0, 1).wait_recv()
+            near_grad(h, i, 1).start()
+
+    def grads_here(u, h):
+        i = u // 2
+        if u == 1:
+            near_grad(h, 0, 1).wait_recv()
+        elif u % 2:
+            near_grad(h, i, 1).wait_recv()
+            far_grad(h, i, 1, 0).wait_recv()
+        elif u:
+            far_grad(h, i, 0, 0).wait_recv()
+
+    spread_grads(0)
 
     total = held[...]
     high = total.astype(jnp.bfloat16)
@@ -420,7 +455,9 @@
         return pl.ds(h * slab, slab)
 
     def back_step(u, h, flipped, d):
-        right = tile_rows(rep_peer(rep_size - u) * blocks, blocks, d * blocks, blocks)
+        from_outer = lax.rem(outer + outer_size - u // 2, outer_size)
+        group = from_outer * 2 + (1 - inner if u % 2 else inner)
+        right = tile_rows(group * blocks, blocks, d * blocks, blocks)
         product = jnp.dot(flipped, right, preferred_element_type=jnp.float32)
         if u > 0:
             product = back[d, slab_of(h), :] + product
@@ -430,8 +467,7 @@
         return jnp.transpose(grads[h, u].astype(jnp.float32)).astype(jnp.bfloat16)
 
     def back_all(u, h):
-        if u > 0:
-            grad_copy(u, h).wait_recv()
+        grads_here(u, h)
         flipped = flip(u, h)
         lax.fori_loop(0, dom_size, lambda d, c: (back_step(u, h, flipped, d), c)[1], 0)
 
@@ -490,7 +526,7 @@
 
     def back_last(h, between):
         u = rep_size - 1
-        grad_copy(u, h).wait_recv()
+        grads_here(u, h)
         flipped = flip(u, h)
 
         def toward(j, carry):
@@ -526,20 +562,20 @@
         lax.fori_loop(0, chips, keep, 0)
 
     ticks = each * (chips - 2)
-    for h in range(HALVES):
-        back_all(0, h)
+    back_all(0, 0)
+    relay_grads(0)
     weight_second()
     for h in range(1, HALVES):
-        for u in range(1, rep_size):
-            grad_copy(u, h).start()
+        spread_grads(h)
     for u in range(1, rep_size - 1):
         back_all(u, 0)
     back_last(0, weight_third)
     for h in range(1, HALVES):
-        for u in range(1, rep_size - 1):
+        relay_grads(h)
+        for u in range(rep_size - 1):
             back_all(u, h)
-            relays(1 + ticks * (u - 1) // (rep_size - 1), 1 + ticks * u // (rep_size - 1), h - 1)
-        back_last(h, lambda: relays(1 + ticks * (rep_size - 2) // (rep_size - 1), 1 + ticks, h - 1))
+            relays(1 + ticks * u // rep_size, 1 + ticks * (u + 1) // rep_size, h - 1)
+        back_last(h, lambda: relays(1 + ticks * (rep_size - 1) // rep_size, 1 + ticks, h - 1))
     relays(1, 1 + ticks, HALVES - 1)
 
     for h in range(HALVES):
@@ -569,14 +605,19 @@
         for k in range(3):
             far_copy(i, k).wait_send()
     for u in range(1, rep_size):
-        for h in range(HALVES):
-            grad_copy(u, h).wait_send()
         gw2_copy(u).wait_send()
     for i in range(1, dom_size):
         gw1_copy(i).wait_send()
         gw3_copy(i).wait_send()
-    for j in range(chips):
-        for h in range(HALVES):
+    for h in range(HALVES):
+        for p in range(2):
+            near_grad(h, 0, p).wait_send()
+        for i in range(1, outer_size):
+            near_grad(h, i, 1).wait_send()
+            far_grad(h, i, 0, 0).wait_send()
+            far_grad(h, i, 0, 1).wait_send()
+            far_grad(h, i, 1, 0).wait_send()
+        for j in range(chips):
             pair_copy(j, h).wait_send()
 
     def sent(q, carry):
@@ -693,7 +734,8 @@
         sems(LOADS), sems(5), sems(3), sems(walks), sems(walks), sems(walks), sems(walks),
         sems(SUB * chips), sems(SUB * chips),
         sems(rep_size // 2 + 1), sems(rep_size // 2 + 1), sems(3 * (rep_size // 2 - 1)), sems(3 * (rep_size // 2 - 1)),
-        sems(HALVES * rep_size), sems(HALVES * rep_size),
+        sems(HALVES * (rep_size // 2 + 1)), sems(HALVES * (rep_size // 2 + 1)),
+        sems(HALVES * 3 * (rep_size // 2 - 1)), sems(HALVES * 3 * (rep_size // 2 - 1)),
         sems(HALVES * chips), sems(HALVES * chips), sems(hops), sems(hops), sems(hops), sems(hops),
         sems(dom_size), sems(dom_size), sems(rep_size), sems(rep_size),
         sems(dom_size), sems(dom_size),

time: 80.2 us -> 78.4 us (0.978)
  Pallas kernels: 76.5 us -> 74.7 us
    pallas_call x1, Pallas kernels: 75.4 us -> 73.6 us  [run_layer(): pl.pallas_call(functools.partial(layer_kernel, dom_size, rep_size), out_s...]
where the time goes in v2:
time: 78.4 us; the launch traced here: 78.2 us
  Pallas kernels  74.7 us (95%)
  local copies, waits for them, and re-layouts  2.26 us (3%)
  between operations  1.3 us (2%)
    pallas_call x1, Pallas kernels, run_layer(): pl.pallas_call(functools.partial(layer_kernel, dom_size, rep_size), out_s...  73.6 us
    unnamed x6, local copies, waits for them, and re-layouts  2.26 us

profile of v2, /device:TPU:0, one launch (start us, length us, event | category | flops | bytes accessed | tf_op | source)
XLA Modules:
  0.0 78.2 jit_solution(16186036317513547495)
XLA Ops:
  1.3 0.0 copy-start
  1.3 0.9 %copy-done = bf16[256,256]{1,0:T(8,128)(2,1)S(1)} copy-done((bf16[256,256]{1,0:T(8,128)(2,1)S(1)}, bf16[256,256]{1,0:T(8,128)(2,1)}, u32[]{:S(2)}) %copy-start) | copy-done | bytes 131096
  2.2 0.0 copy-start.1
  2.2 0.7 copy-done.1
  2.9 0.0 copy-start.2
  2.9 0.7 copy-done.2
  3.5 73.6 %layer.1 = (bf16[512,256]{1,0:T(8,128)(2,1)S(1)}, bf16[256,512]{1,0:T(8,128)(2,1)S(1)}, bf16[256,256]{1,0:T(8,128)(2,1)S(1)}) custom-call(s32[1]{0:T(128)} %bitcast.4.refs_0_, bf16[512,256]{1,0:T(8,128)(2,1)} %refs_1_.1, bf16[256,256]{1,0:T(8,128)(2,1)S(1)} %copy-done, bf16[512,256]{1,0:T(8,128)(2,1)} %refs_3_.1, s32[1,512]{1,0:T(1,128)S(1)} %bitcast.5, ...), custom_call_target="tpu_custom_call" | custom-call | tf_op jit(solution)/shard_map/layer/pallas_call | solution.py:743
  77.2 1.1 %finish.1 = (bf16[512,256]{1,0:T(8,128)(2,1)}, bf16[512,256]{1,0:T(8,128)(2,1)}, f32[256,256]{1,0:T(8,128)}) custom-call(bf16[512,256]{1,0:T(8,128)(2,1)S(1)} %get-tuple-element.6.raw_ref, bf16[256,512]{1,0:T(8,128)(2,1)S(1)} %get-tuple-element.7.gp_ref, bf16[256,256]{1,0:T(8,128)(2,1)S(1)} %get-tuple-element.8.gw_in_ref, bf16[256,256]{1,0:T(8,128)(2,1)S(1)} %copy-done), custom_call_target="tpu_custom_call" | custom-call | tf_op jit(solution)/shard_map/finish/pallas_call | solution.py:665
Async XLA Ops:
  1.3 0.9 %copy-start = (bf16[256,256]{1,0:T(8,128)(2,1)S(1)}, bf16[256,256]{1,0:T(8,128)(2,1)}, u32[]{:S(2)}) copy-start(bf16[256,256]{1,0:T(8,128)(2,1)} %weight_ref.1) | copy-start | bytes 393220
  2.2 0.7 copy-start.1
  2.9 0.7 copy-start.2
